TPU v7x, 32 devices: a whole 2x2x4 slice. The times are simulated.
32 devices in a mesh: dp: 2 (over x), fsdp: 8 (over z, y), seq: 2 (over core).
Axes of the slice: x: 2, y: 2, z: 4, core: 2. Of those that a mesh axis runs over, the one named last changes fastest.
Arguments:
- tokens_in: bfloat16 [16, 1040, 1024], P(('dp', 'fsdp'), 'seq'), may hold values from -6 to 6
- key_mask: int32 [16, 1040], P(('dp', 'fsdp')), may hold values from 0 to 1, as said below
- attn_weights: bfloat16 [2, 1024, 4096], P(None, 'fsdp')
- mlp_weights: bfloat16 [2, 1024, 8192], P(None, 'fsdp')
- vectors: bfloat16 [2, 14, 1024], P(None, None, 'fsdp')
- cotangent: bfloat16 [16, 1040, 1024], P(('dp', 'fsdp'), 'seq'), may hold values from -6 to 6
- first_attn: float32 [2, 1024, 4096], P(None, 'fsdp'), may hold values from -40 to 40
- second_attn: float32 [2, 1024, 4096], P(None, 'fsdp'), may hold values from 0.832 to 8.32
- first_mlp: float32 [2, 1024, 8192], P(None, 'fsdp'), may hold values from -40 to 40
- second_mlp: float32 [2, 1024, 8192], P(None, 'fsdp'), may hold values from 0.832 to 8.32
- first_vec: float32 [2, 14, 1024], P(None, None, 'fsdp'), may hold values from -80 to 80
- second_vec: float32 [2, 14, 1024], P(None, None, 'fsdp'), may hold values from 3.328 to 33.28
Outputs:
- tokens_out: float32 [16, 1040, 1024], P(('dp', 'fsdp'), 'seq')
- grad_tokens: float32 [16, 1040, 1024], P(('dp', 'fsdp'), 'seq')
- grad_attn: float32 [2, 1024, 4096], P(None, 'fsdp')
- grad_mlp: float32 [2, 1024, 8192], P(None, 'fsdp')
- grad_vectors: float32 [2, 14, 1024], P(None, None, 'fsdp')
- step_attn: float32 [2, 1024, 4096], P(None, 'fsdp')
- step_mlp: float32 [2, 1024, 8192], P(None, 'fsdp')
- step_vectors: float32 [2, 14, 1024], P(None, None, 'fsdp')
- new_first_attn: float32 [2, 1024, 4096], P(None, 'fsdp')
- new_second_attn: float32 [2, 1024, 4096], P(None, 'fsdp')
- new_first_mlp: float32 [2, 1024, 8192], P(None, 'fsdp')
- new_second_mlp: float32 [2, 1024, 8192], P(None, 'fsdp')
- new_first_vec: float32 [2, 14, 1024], P(None, None, 'fsdp')
- new_second_vec: float32 [2, 14, 1024], P(None, None, 'fsdp')
Inputs may be any that keep to these rules, and one draw needn't show every extreme that they name: `key_mask`: each image's row is 1 on its first slots and 0 on the rest; at least 910 ones and at least one 0 in every row.
All inputs are finite; a program needn't handle non-finite values.
Results may differ from a plain program's by a relative error of at most 0.023.
Values may be sent and summed in bfloat16 or wider, within the bound.
No kernel may reach another device: no remote copies, remote signals or barrier semaphores. Data moves between devices by JAX's collectives and lax.ppermute only.
A program may use at most 320 MiB of HBM per device.

v0:
```python
import jax
import jax.numpy as jnp
from jax import lax
from jax.sharding import PartitionSpec as P

HD = 64
norm_eps = 1e-06
neg_large = -1e30
beta_first = 0.9
beta_second = 0.999
adam_eps = 1e-08
decay_rate = 0.05
rate_matrix = 0.01
rate_vector = 0.05
step_count = 10.0


def layer_norm(values, norm_gain, norm_shift):
    center = values - jnp.mean(values, axis=-1, keepdims=True)
    spread = jnp.mean(center * center, axis=-1, keepdims=True)
    return center * lax.rsqrt(spread + norm_eps) * norm_gain + norm_shift


def gelu_exact(values):
    return jax.nn.gelu(values, approximate=False)


def contract_last(left_side, right_side):
    return lax.dot_general(
        left_side,
        right_side,
        (((left_side.ndim - 1,), (1,)), ((), ())),
        preferred_element_type=jnp.float32,
    )


def contract_rows(left_side, right_side):
    return lax.dot_general(
        left_side, right_side, (((0, 1), (0, 1)), ((), ())), preferred_element_type=jnp.float32
    )


def masked_scores(query_rows, key_rows, valid_keys):
    scores = contract_last(query_rows, key_rows) * query_rows.shape[-1] ** (-0.5)
    return jnp.where(valid_keys[None, :] > 0, scores, neg_large)


def attend_item(item_set):
    query_rows, key_rows, value_rows, valid_keys = item_set
    scores = masked_scores(query_rows, key_rows, valid_keys)
    row_top = jnp.max(scores, axis=-1, keepdims=True)
    exp_terms = jnp.exp(scores - row_top)
    row_total = jnp.sum(exp_terms, axis=-1, keepdims=True)
    attention = (exp_terms / row_total).astype(jnp.bfloat16)
    mixed_rows = jnp.dot(attention, value_rows, preferred_element_type=jnp.float32)
    return (mixed_rows.astype(jnp.bfloat16), row_top[:, 0] + jnp.log(row_total[:, 0]))


def attend_back(item_set):
    query_rows, key_rows, value_rows, valid_keys, log_total, grad_rows = item_set
    score_scale = query_rows.shape[-1] ** (-0.5)
    scores = masked_scores(query_rows, key_rows, valid_keys)
    attention = jnp.exp(scores - log_total[:, None])
    grad_value = lax.dot_general(
        attention.astype(jnp.bfloat16),
        grad_rows,
        (((0,), (0,)), ((), ())),
        preferred_element_type=jnp.float32,
    )
    grad_attention = contract_last(grad_rows, value_rows)
    inner_sum = jnp.sum(attention * grad_attention, axis=-1, keepdims=True)
    grad_scores = (attention * (grad_attention - inner_sum)).astype(jnp.bfloat16)
    grad_query = jnp.dot(grad_scores, key_rows, preferred_element_type=jnp.float32) * score_scale
    grad_key = (
        lax.dot_general(
            grad_scores, query_rows, (((0,), (0,)), ((), ())), preferred_element_type=jnp.float32
        )
        * score_scale
    )
    return jnp.stack([grad_query, grad_key, grad_value]).astype(jnp.bfloat16)


def forward_layer(inputs, mask_heads, attn_full, mlp_full, vectors_full):
    model_width = attn_full.shape[0]
    hidden = mlp_full.shape[1] // 2
    vec_rows = vectors_full.astype(jnp.float32)
    n_seq = lax.axis_size("seq")
    images, token_rows, _ = inputs.shape
    length = token_rows * n_seq
    group_width = model_width // n_seq
    per_group = group_width // HD
    normed = layer_norm(inputs, vec_rows[0], vec_rows[1]).astype(jnp.bfloat16)
    bias_qkv = jnp.concatenate([vec_rows[2], jnp.zeros_like(vec_rows[2]), vec_rows[3]])
    qkv = (
        jnp.dot(normed, attn_full[:, : 3 * model_width], preferred_element_type=jnp.float32)
        + bias_qkv
    ).astype(jnp.bfloat16)
    heads = lax.all_to_all(
        qkv.reshape(images, token_rows, 3, n_seq, group_width),
        "seq",
        split_axis=3,
        concat_axis=1,
        tiled=True,
    )
    stacked = (
        heads.reshape(images, length, 3, per_group, HD)
        .transpose(2, 0, 3, 1, 4)
        .reshape(3, images * per_group, length, HD)
    )
    mixed_items, log_total = lax.map(attend_item, (stacked[0], stacked[1], stacked[2], mask_heads))
    mixed_heads = (
        mixed_items.reshape(images, per_group, length, HD)
        .transpose(0, 2, 1, 3)
        .reshape(images, length, 1, group_width)
    )
    mixed_rows = lax.all_to_all(
        mixed_heads, "seq", split_axis=1, concat_axis=2, tiled=True
    ).reshape(images, token_rows, model_width)
    branch = contract_last(mixed_rows, attn_full[:, 3 * model_width :]) + vec_rows[4]
    middle = inputs + vec_rows[5] * branch
    normed_two = layer_norm(middle, vec_rows[6], vec_rows[7]).astype(jnp.bfloat16)
    pre_act = jnp.dot(
        normed_two, mlp_full[:, :hidden], preferred_element_type=jnp.float32
    ) + vec_rows[10:].reshape(hidden)
    active = gelu_exact(pre_act).astype(jnp.bfloat16)
    mlp_out = contract_last(active, mlp_full[:, hidden:]) + vec_rows[8]
    output = middle + vec_rows[9] * mlp_out
    saved_set = (
        inputs,
        normed,
        stacked,
        log_total,
        mixed_rows,
        branch,
        middle,
        normed_two,
        pre_act,
        active,
        mlp_out,
    )
    return (output, saved_set)


def backward_layer(upstream, saved_set, attn_full, mlp_full, vectors_full, mask_heads):
    (
        inputs,
        normed,
        stacked,
        log_total,
        mixed_rows,
        branch,
        middle,
        normed_two,
        pre_act,
        active,
        mlp_out,
    ) = saved_set
    model_width = attn_full.shape[0]
    hidden = mlp_full.shape[1] // 2
    vec_rows = vectors_full.astype(jnp.float32)
    n_seq = lax.axis_size("seq")
    images, token_rows, _ = upstream.shape
    length = token_rows * n_seq
    group_width = model_width // n_seq
    per_group = group_width // HD
    grad_scale_two = jnp.sum(upstream * mlp_out, axis=(0, 1))
    grad_mlp_out = (upstream * vec_rows[9]).astype(jnp.bfloat16)
    grad_bias_down = jnp.sum(grad_mlp_out.astype(jnp.float32), axis=(0, 1))
    grad_down = contract_rows(grad_mlp_out, active)
    grad_active = jnp.dot(grad_mlp_out, mlp_full[:, hidden:], preferred_element_type=jnp.float32)
    _, gelu_pull = jax.vjp(gelu_exact, pre_act)
    grad_pre = gelu_pull(grad_active)[0].astype(jnp.bfloat16)
    grad_bias_up = jnp.sum(grad_pre.astype(jnp.float32), axis=(0, 1))
    grad_up = contract_rows(normed_two, grad_pre)
    grad_normed_two = contract_last(grad_pre, mlp_full[:, :hidden])
    _, second_pull = jax.vjp(layer_norm, middle, vec_rows[6], vec_rows[7])
    grad_mid_norm, grad_gain_two, grad_shift_two = second_pull(grad_normed_two)
    grad_middle = upstream + grad_mid_norm
    grad_scale_one = jnp.sum(grad_middle * branch, axis=(0, 1))
    grad_branch = (grad_middle * vec_rows[5]).astype(jnp.bfloat16)
    grad_bias_proj = jnp.sum(grad_branch.astype(jnp.float32), axis=(0, 1))
    grad_proj = contract_rows(grad_branch, mixed_rows)
    grad_mixed = jnp.dot(
        grad_branch, attn_full[:, 3 * model_width :], preferred_element_type=jnp.float32
    ).astype(jnp.bfloat16)
    grad_heads = lax.all_to_all(
        grad_mixed.reshape(images, token_rows, n_seq, group_width),
        "seq",
        split_axis=2,
        concat_axis=1,
        tiled=True,
    )
    grad_items = (
        grad_heads.reshape(images, length, per_group, HD)
        .transpose(0, 2, 1, 3)
        .reshape(images * per_group, length, HD)
    )
    grad_stack = lax.map(
        attend_back, (stacked[0], stacked[1], stacked[2], mask_heads, log_total, grad_items)
    )
    grad_stack = (
        grad_stack.reshape(images, per_group, 3, length, HD)
        .transpose(0, 3, 2, 1, 4)
        .reshape(images, length, 3, 1, group_width)
    )
    grad_qkv = lax.all_to_all(grad_stack, "seq", split_axis=1, concat_axis=3, tiled=True).reshape(
        images, token_rows, 3 * model_width
    )
    grad_qkv_sum = jnp.sum(grad_qkv.astype(jnp.float32), axis=(0, 1))
    grad_qkv_weight = contract_rows(normed, grad_qkv)
    grad_normed = contract_last(grad_qkv, attn_full[:, : 3 * model_width])
    _, first_pull = jax.vjp(layer_norm, inputs, vec_rows[0], vec_rows[1])
    grad_in_norm, grad_gain_one, grad_shift_one = first_pull(grad_normed)
    grad_inputs = grad_middle + grad_in_norm
    grad_attn = jnp.concatenate([grad_qkv_weight, grad_proj], axis=1)
    grad_mlp = jnp.concatenate([grad_up, grad_down], axis=1)
    grad_rows = jnp.stack(
        [
            grad_gain_one,
            grad_shift_one,
            grad_qkv_sum[:model_width],
            grad_qkv_sum[2 * model_width :],
            grad_bias_proj,
            grad_scale_one,
            grad_gain_two,
            grad_shift_two,
            grad_bias_down,
            grad_scale_two,
        ]
    )
    grad_vec = jnp.concatenate(
        [grad_rows, grad_bias_up.reshape(hidden // model_width, model_width)], axis=0
    )
    return (grad_inputs, (grad_attn, grad_mlp, grad_vec))


def adam_step(weights, gradient, moment_one, moment_two, step_rate, decay_weight):
    one_new = beta_first * moment_one + (1.0 - beta_first) * gradient
    two_new = beta_second * moment_two + (1.0 - beta_second) * gradient * gradient
    one_hat = one_new / (1.0 - beta_first**step_count)
    two_hat = two_new / (1.0 - beta_second**step_count)
    change = -step_rate * (
        one_hat / (jnp.sqrt(two_hat) + adam_eps) + decay_weight * weights.astype(jnp.float32)
    )
    return (change, one_new, two_new)


def local(
    tokens_in,
    key_mask,
    attn_weights,
    mlp_weights,
    vectors,
    cotangent,
    first_attn,
    second_attn,
    first_mlp,
    second_mlp,
    first_vec,
    second_vec,
):
    layers = attn_weights.shape[0]
    n_seq = lax.axis_size("seq")
    per_group = attn_weights.shape[2] // 4 // n_seq // HD
    mask_heads = jnp.repeat(key_mask, per_group, axis=0)
    residual = tokens_in.astype(jnp.float32)
    stored = []
    gathered_sets = []
    for layer_index in range(layers):
        weight_set = (
            lax.all_gather(attn_weights[layer_index], "fsdp", axis=0, tiled=True),
            lax.all_gather(mlp_weights[layer_index], "fsdp", axis=0, tiled=True),
            lax.all_gather(vectors[layer_index], "fsdp", axis=1, tiled=True),
        )
        residual, saved_set = forward_layer(
            residual, mask_heads, weight_set[0], weight_set[1], weight_set[2]
        )
        stored.append(saved_set)
        gathered_sets.append(weight_set)
    upstream = cotangent.astype(jnp.float32)
    layer_grads = [None] * layers
    for layer_index in reversed(range(layers)):
        weight_set = (
            lax.all_gather(attn_weights[layer_index], "fsdp", axis=0, tiled=True),
            lax.all_gather(mlp_weights[layer_index], "fsdp", axis=0, tiled=True),
            lax.all_gather(vectors[layer_index], "fsdp", axis=1, tiled=True),
        )
        upstream, local_grads = backward_layer(
            upstream, stored[layer_index], weight_set[0], weight_set[1], weight_set[2], mask_heads
        )
        owned = (
            lax.psum_scatter(
                local_grads[0].astype(jnp.bfloat16), "fsdp", scatter_dimension=0, tiled=True
            ).astype(jnp.float32),
            lax.psum_scatter(
                local_grads[1].astype(jnp.bfloat16), "fsdp", scatter_dimension=0, tiled=True
            ).astype(jnp.float32),
            lax.psum_scatter(
                local_grads[2].astype(jnp.bfloat16), "fsdp", scatter_dimension=1, tiled=True
            ).astype(jnp.float32),
        )
        owned = (
            lax.psum(owned[0].astype(jnp.bfloat16), ("dp", "seq")).astype(jnp.float32),
            lax.psum(owned[1].astype(jnp.bfloat16), ("dp", "seq")).astype(jnp.float32),
            lax.psum(owned[2].astype(jnp.bfloat16), ("dp", "seq")).astype(jnp.float32),
        )
        layer_grads[layer_index] = owned
    grad_attn = jnp.stack([layer_grads[index_one][0] for index_one in range(layers)])
    grad_mlp = jnp.stack([layer_grads[index_one][1] for index_one in range(layers)])
    grad_vectors = jnp.stack([layer_grads[index_one][2] for index_one in range(layers)])
    step_attn, one_attn, two_attn = adam_step(
        attn_weights, grad_attn, first_attn, second_attn, rate_matrix, decay_rate
    )
    step_mlp, one_mlp, two_mlp = adam_step(
        mlp_weights, grad_mlp, first_mlp, second_mlp, rate_matrix, decay_rate
    )
    step_vectors, one_vec, two_vec = adam_step(
        vectors, grad_vectors, first_vec, second_vec, rate_vector, 0.0
    )
    return (
        residual,
        upstream,
        grad_attn,
        grad_mlp,
        grad_vectors,
        step_attn,
        step_mlp,
        step_vectors,
        one_attn,
        two_attn,
        one_mlp,
        two_mlp,
        one_vec,
        two_vec,
    )


def solution(mesh):
    return jax.shard_map(
        local,
        mesh=mesh,
        in_specs=(
            P(("dp", "fsdp"), "seq", None),
            P(("dp", "fsdp"), None),
            P(None, "fsdp", None),
            P(None, "fsdp", None),
            P(None, None, "fsdp"),
            P(("dp", "fsdp"), "seq", None),
            P(None, "fsdp", None),
            P(None, "fsdp", None),
            P(None, "fsdp", None),
            P(None, "fsdp", None),
            P(None, None, "fsdp"),
            P(None, None, "fsdp"),
        ),
        out_specs=(
            P(("dp", "fsdp"), "seq", None),
            P(("dp", "fsdp"), "seq", None),
            P(None, "fsdp", None),
            P(None, "fsdp", None),
            P(None, None, "fsdp"),
            P(None, "fsdp", None),
            P(None, "fsdp", None),
            P(None, None, "fsdp"),
            P(None, "fsdp", None),
            P(None, "fsdp", None),
            P(None, "fsdp", None),
            P(None, "fsdp", None),
            P(None, None, "fsdp"),
            P(None, None, "fsdp"),
        ),
        check_vma=False,
    )
```

profile of v0, /device:TPU:0, one launch (start us, length us, event | category | flops | bytes accessed | tf_op | source)
XLA Modules:
  0.0 2304.5 jit_solution(1958127319763447503)
XLA Ops:
  16.5 23.2 %all-gather = bf16[1,14,1024]{2,0,1:T(2,128)(2,1)S(1)} all-gather(bf16[1,14,128]{2,0,1:T(2,128)(2,1)S(1)} %get-tuple-element.468), channel_id=2, replica_groups=mesh['dp'=2,'fsdp'=8,'seq'=2] {'fsdp'}, dimensions={2}, use_global_device_ids=true | all-gather | bytes 32256 | tf_op jit(solution)/shard_map/all_gather | solution.py:273
  39.9 17.4 all-gather.3
  59.9 79.7 %all-gather.11.cloned.1.call-done = bf16[1,1024,4096]{2,1,0:T(8,128)(2,1)} async-done(((bf16[1,128,4096]{2,1,0:T(8,128)(2,1)}), bf16[1,1024,4096]{2,1,0:T(8,128)(2,1)}) %all-gather.11.cloned.1.call-update) | async-done | bytes 8388624 | tf_op jit(solution)/shard_map/all_gather | solution.py:271
  139.5 8.1 add_convert_fusion.3
  147.6 8.5 reshape.862
  158.6 7.5 all_to_all.120
  166.1 10.3 copy.103
  176.4 8.6 reshape.863
  198.8 72.4 %while.44 = (s32[]{:T(128)}, bf16[8,1040,64]{1,2,0:T(8,128)(2,1)}, f32[8,1040]{1,0:T(8,128)S(1)}, s32[8,1040]{1,0:T(8,128)S(1)}, bf16[8,1040,64]{2,1,0:T(8,128)(...) while((s32[]{:T(128)}, bf16[8,1040,64]{1,2,0:T(8,128)(2,1)}, ...), condition=%wide.region_5.6_spmd, body=%wide.region_2.5_spmd.sunk | while | flops 285608960 | bytes 31756240 | solution.py:110
  271.2 6.4 copy.107
  278.2 8.9 reduce.63
  289.4 7.1 all_to_all.121
  299.9 4.7 fusion.226
  305.0 63.0 %all-gather.13.cloned.1.call-done = bf16[1,1024,8192]{2,1,0:T(8,128)(2,1)} async-done(((bf16[1,128,8192]{2,1,0:T(8,128)(2,1)}), bf16[1,1024,8192]{2,1,0:T(8,128)(2,1)}) %all-gather.13.cloned.1.call-update) | async-done | bytes 16777232 | tf_op jit(solution)/shard_map/all_gather | solution.py:272
  368.1 27.1 %multiply_convert_fusion.3 = (bf16[520,4096]{1,0:T(8,128)(2,1)S(1)}, f32[520,4096]{1,0:T(8,128)}, f32[520,4096]{1,0:T(8,128)}) fusion(f32[4096]{0:T(1024)S(1)} %bitcast.487, bf16[1024,8192]{1,0:T(8,128)(2,1)} %bitcast.522, f32[1,520,1024]{2,1,0:T(8,128)S(1)} %get-tuple-element.424, f32[1024]{0:T(1024)S(1)} %bitcast.513, f32[1024]{0:T(1024)S(1)} %bitcast.499, ...), kind=kOutput, calls=%fused_computation.138 | convolution fusion | flops 4505313280 | bytes 31846464 | tf_op jit(solution)/shard_map/dot_general | solution.py:122
  395.3 11.5 fusion.224
  407.2 86.7 %all-gather.15.cloned.1.call-done = bf16[1,1024,4096]{2,1,0:T(8,128)(2,1)} async-done(((bf16[1,128,4096]{2,1,0:T(8,128)(2,1)}), bf16[1,1024,4096]{2,1,0:T(8,128)(2,1)}) %all-gather.15.cloned.1.call-update) | async-done | bytes 8388624 | tf_op jit(solution)/shard_map/all_gather | solution.py:271
  493.9 8.0 add_convert_fusion.2
  502.0 8.6 reshape.869
  513.0 7.5 all_to_all.122
  520.5 10.3 copy.110
  530.7 8.6 reshape.870
  552.9 68.8 %while.45 = (s32[]{:T(128)}, bf16[8,1040,64]{1,2,0:T(8,128)(2,1)S(1)}, f32[8,1040]{1,0:T(8,128)S(1)}, s32[8,1040]{1,0:T(8,128)S(1)}, bf16[8,1040,64]{2,1,0:T(8,1...) while((s32[]{:T(128)}, ...), condition=%wide.region_13.14_spmd, body=%wide.region_10.13_spmd.sunk | while | flops 285608960 | bytes 31763296 | solution.py:110
  625.8 8.9 reduce.64
  636.2 5.6 all_to_all.123
  647.8 4.7 fusion.223
  654.4 67.8 %all-gather.17.cloned.1.call-done = bf16[1,1024,8192]{2,1,0:T(8,128)(2,1)} async-done(((bf16[1,128,8192]{2,1,0:T(8,128)(2,1)}), bf16[1,1024,8192]{2,1,0:T(8,128)(2,1)}) %all-gather.17.cloned.1.call-update) | async-done | bytes 16777232 | tf_op jit(solution)/shard_map/all_gather | solution.py:272
  722.3 28.0 %multiply_convert_fusion.2 = (bf16[520,4096]{1,0:T(8,128)(2,1)}, f32[520,4096]{1,0:T(8,128)}, f32[520,4096]{1,0:T(8,128)}) fusion(f32[4096]{0:T(1024)S(1)} %bitcast.489, bf16[1024,8192]{1,0:T(8,128)(2,1)} %bitcast.526, f32[1,520,1024]{2,1,0:T(8,128)} %copy-done.8, f32[1024]{0:T(1024)S(1)} %bitcast.511, f32[1024]{0:T(1024)S(1)} %bitcast.495, ...), kind=kOutput, calls=%fused_computation.125 | convolution fusion | flops 4505313280 | bytes 31846464 | tf_op jit(solution)/shard_map/dot_general | solution.py:122
  750.4 14.5 fusion.234
  764.9 9.6 fusion.153
  792.1 99.1 %while.46 = (s32[]{:T(128)}, bf16[8,3,1040,64]{2,3,1,0:T(8,128)(2,1)S(1)}, s32[8,1040]{1,0:T(8,128)}, bf16[8,1040,64]{2,1,0:T(8,128)(2,1)}, bf16[8,1040,64]{2,1,...) while((s32[]{:T(128)}, ...), condition=%wide.region_20.21_spmd, body=%wide.region_18.20_spmd.sunk | while | flops 703489280 | bytes 35388936 | solution.py:198
  893.3 8.4 copy.123
  901.8 8.7 all_to_all.125
  917.1 8.5 reshape.882
  925.7 7.9 fusion.155
  937.0 14.5 fusion.152
  952.4 14.3 fusion.235
  966.7 10.0 fusion.157
  997.4 99.1 %while.47 = (s32[]{:T(128)}, bf16[8,3,1040,64]{2,3,1,0:T(8,128)(2,1)S(1)}, s32[8,1040]{1,0:T(8,128)}, bf16[8,1040,64]{2,1,0:T(8,128)(2,1)}, bf16[8,1040,64]{2,1,...) while((s32[]{:T(128)}, ...), condition=%wide.region_27.28_spmd, body=%wide.region_25.27_spmd.sunk | while | flops 703489280 | bytes 35388936 | solution.py:198
  1098.7 8.4 copy.133
  1107.1 8.7 all_to_all.127
  1122.4 8.4 reshape.890
  1130.9 9.4 convolution_convert_fusion.5
  1140.3 7.0 pad_maximum_fusion.2
  1147.4 4.9 convolution_convert_fusion.6
  1152.3 7.7 convolution_convert_fusion.4
  1160.1 7.8 pad_maximum_fusion.3
  1167.9 9.1 convolution_convert_fusion.2
  1177.0 9.6 convolution_convert_fusion.3
  1186.6 6.6 pad_maximum_fusion
  1193.9 9.3 convolution_convert_fusion
  1203.3 9.6 convolution_convert_fusion.1
  1212.9 6.6 pad_maximum_fusion.1
  1219.6 6.9 fusion.150
  1237.8 56.8 %reduce-scatter.11.cloned.1.call-done = bf16[128,4096]{1,0:T(8,128)(2,1)} async-done(((bf16[1024,4096]{1,0:T(8,128)(2,1)}), bf16[128,4096]{1,0:T(8,128)(2,1)}) %reduce-scatter.11.cloned.1.call-update) | async-done | bytes 1048592 | tf_op jit(solution)/shard_map/reduce_scatter | solution.py:292
  1294.7 152.5 %reduce-scatter.13.cloned.1.call-done = bf16[128,4096]{1,0:T(8,128)(2,1)} async-done(((bf16[1024,4096]{1,0:T(8,128)(2,1)}), bf16[128,4096]{1,0:T(8,128)(2,1)}) %reduce-scatter.13.cloned.1.call-update) | async-done | bytes 1048592 | tf_op jit(solution)/shard_map/reduce_scatter | solution.py:292
  1447.2 285.6 %reduce-scatter.15.cloned.1.call-done = bf16[128,8192]{1,0:T(8,128)(2,1)} async-done(((bf16[1024,8192]{1,0:T(8,128)(2,1)}), bf16[128,8192]{1,0:T(8,128)(2,1)}) %reduce-scatter.15.cloned.1.call-update) | async-done | bytes 2097168 | tf_op jit(solution)/shard_map/reduce_scatter | solution.py:295
  1732.8 286.1 %reduce-scatter.17.cloned.1.call-done = bf16[128,8192]{1,0:T(8,128)(2,1)} async-done(((bf16[1024,8192]{1,0:T(8,128)(2,1)}), bf16[128,8192]{1,0:T(8,128)(2,1)}) %reduce-scatter.17.cloned.1.call-update) | async-done | bytes 2097168 | tf_op jit(solution)/shard_map/reduce_scatter | solution.py:295
  2022.6 60.4 %reduce-scatter.19.cloned.1.call-done = bf16[128,14]{1,0:T(8,128)(2,1)} async-done(((bf16[1024,14]{1,0:T(8,128)(2,1)}), bf16[128,14]{1,0:T(8,128)(2,1)}) %reduce-scatter.19.cloned.1.call-update) | async-done | bytes 3600
  2083.9 63.2 %reduce-scatter.21.cloned.1.call-done = bf16[128,14]{1,0:T(8,128)(2,1)} async-done(((bf16[1024,14]{1,0:T(8,128)(2,1)}), bf16[128,14]{1,0:T(8,128)(2,1)}) %reduce-scatter.21.cloned.1.call-update) | async-done | bytes 3600
  2147.9 5.8 all-reduce
  2156.2 112.7 %all-reduce.4.cloned.1.call-done = (bf16[1,128,4096]{2,1,0:T(8,128)(2,1)}, bf16[1,128,4096]{2,1,0:T(8,128)(2,1)}, bf16[1,128,8192]{2,1,0:T(8,128)(2,1)}, bf16[1,128,8192]{2,1,0:T(8,128)(2,1)}) async-done(((bf16[1,128,4096]{2,1,0:T(8,128)(2,1)}, bf16[1,128,4096]{2,1,0:T(8,128)(2,1)}, bf16[1,128,8192]{2,1,0:T(8,128)(2,1)}, bf16[1,128,8192]{2,1,0:T(8,128)(2,1)}), (bf16[1,128,4096]{2,1,0:T(8,128)(2,1)}, ...) | async-done | bytes 6291472 | tf_op jit(solution)/shard_map/psum | solution.py:303
  2268.9 19.0 add_multiply_fusion
  2288.0 9.8 add_multiply_fusion.1
  (680 shorter events, 481.9 us)
Async XLA Ops:
  7.2 132.3 %all-gather.11.cloned.1.call-start = ((), (), s32[]{:S(2)}) async-start(), calls=%async_computation.18 | async-start | bytes 9437184 | tf_op jit(solution)/shard_map/all_gather | solution.py:271
  10.3 357.7 %all-gather.13.cloned.1.call-start = ((), (), s32[]{:S(2)}) async-start(), calls=%async_computation.19 | async-start | bytes 18874368 | tf_op jit(solution)/shard_map/all_gather | solution.py:272
  15.1 43.5 %copy-start.16 = (bf16[1,520,1024]{2,1,0:T(8,128)(2,1)S(1)}, bf16[1,520,1024]{2,1,0:T(8,128)(2,1)}, u32[]{:S(2)}) copy-start(bf16[1,520,1024]{2,1,0:T(8,128)(2,1)} %param.20) | copy-start | bytes 3194884
  15.1 44.1 %copy-start.101 = (s32[1,1040]{1,0:T(1,128)S(1)}, s32[1,1040]{1,0:T(1,128)}, u32[]{:S(2)}) copy-start(s32[1,1040]{1,0:T(1,128)} %param.21) | copy-start | bytes 12484
  15.1 478.8 %all-gather.15.cloned.1.call-start = ((), (), s32[]{:S(2)}) async-start(), calls=%async_computation.20 | async-start | bytes 9437184 | tf_op jit(solution)/shard_map/all_gather | solution.py:271
  15.8 706.5 %all-gather.17.cloned.1.call-start = ((), (), s32[]{:S(2)}) async-start(), calls=%async_computation.21 | async-start | bytes 18874368 | tf_op jit(solution)/shard_map/all_gather | solution.py:272
  16.4 1278.3 %reduce-scatter.11.cloned.1.call-start = ((), (), s32[]{:S(2)}) async-start(), calls=%async_computation.14 | async-start | bytes 9437184 | tf_op jit(solution)/shard_map/reduce_scatter | solution.py:292
  39.7 107.9 %copy-start.49 = (f32[1,1,1024]{2,0,1:T(1,128)}, f32[1,1,1024]{2,0,1:T(1,128)S(1)}, u32[]{:S(2)}) copy-start(f32[1,1,1024]{2,0,1:T(1,128)S(1)} %get-tuple-element.463) | copy-start | bytes 12292
  39.8 107.8 %copy-start.106 = (f32[1,1,1024]{2,0,1:T(1,128)}, f32[1,1,1024]{2,0,1:T(1,128)S(1)}, u32[]{:S(2)}) copy-start(f32[1,1,1024]{2,0,1:T(1,128)S(1)} %get-tuple-element.464) | copy-start | bytes 12292
  39.8 260.1 %copy-start.66 = (f32[1,1,1024]{2,0,1:T(1,128)}, f32[1,1,1024]{2,0,1:T(1,128)S(1)}, u32[]{:S(2)}) copy-start(f32[1,1,1024]{2,0,1:T(1,128)S(1)} %get-tuple-element.461) | copy-start | bytes 12292
  39.8 260.1 %copy-start.68 = (f32[1,1,1024]{2,0,1:T(1,128)}, f32[1,1,1024]{2,0,1:T(1,128)S(1)}, u32[]{:S(2)}) copy-start(f32[1,1,1024]{2,0,1:T(1,128)S(1)} %get-tuple-element.462) | copy-start | bytes 12292
  39.8 328.3 %copy-start.77 = (f32[1,1,1024]{2,0,1:T(1,128)}, f32[1,1,1024]{2,0,1:T(1,128)S(1)}, u32[]{:S(2)}) copy-start(f32[1,1,1024]{2,0,1:T(1,128)S(1)} %get-tuple-element.459) | copy-start | bytes 12292
  39.8 328.3 %copy-start.104 = (f32[1,1,1024]{2,0,1:T(1,128)}, f32[1,1,1024]{2,0,1:T(1,128)S(1)}, u32[]{:S(2)}) copy-start(f32[1,1,1024]{2,0,1:T(1,128)S(1)} %get-tuple-element.460) | copy-start | bytes 12292
  39.8 355.4 %copy-start.70 = (f32[1,1,1024]{2,0,1:T(1,128)}, f32[1,1,1024]{2,0,1:T(1,128)S(1)}, u32[]{:S(2)}) copy-start(f32[1,1,1024]{2,0,1:T(1,128)S(1)} %get-tuple-element.457) | copy-start | bytes 12292
  39.8 355.4 %copy-start.110 = (f32[1,1,1024]{2,0,1:T(1,128)}, f32[1,1,1024]{2,0,1:T(1,128)S(1)}, u32[]{:S(2)}) copy-start(f32[1,1,1024]{2,0,1:T(1,128)S(1)} %get-tuple-element.458) | copy-start | bytes 12292
  39.9 328.2 %copy-start.72 = (f32[1,4,1024]{2,0,1:T(1,128)}, f32[1,4,1024]{2,0,1:T(1,128)S(1)}, u32[]{:S(2)}) copy-start(f32[1,4,1024]{2,0,1:T(1,128)S(1)} %slice.263) | copy-start | bytes 49156
  58.7 88.9 %copy-start.42 = (f32[520]{0:T(1024)}, f32[520]{0:T(1024)S(1)}, u32[]{:S(2)}) copy-start(f32[520]{0:T(1024)S(1)} %broadcast_multiply_fusion.3) | copy-start | bytes 6244
  59.2 88.4 %copy-start.51 = (f32[520]{0:T(1024)}, f32[520]{0:T(1024)S(1)}, u32[]{:S(2)}) copy-start(f32[520]{0:T(1024)S(1)} %fusion.149) | copy-start | bytes 6244
  59.2 88.4 %copy-start.44 = (f32[520]{0:T(1024)}, f32[520]{0:T(1024)S(1)}, u32[]{:S(2)}) copy-start(f32[520]{0:T(1024)S(1)} %fusion.199) | copy-start | bytes 6244
  271.2 15.9 copy-start.15
  271.2 15.9 copy-start.40
  304.6 90.6 %copy-start.19 = (f32[1,520,1024]{2,1,0:T(8,128)}, f32[1,520,1024]{2,1,0:T(8,128)S(1)}, u32[]{:S(2)}) copy-start(f32[1,520,1024]{2,1,0:T(8,128)S(1)} %get-tuple-element.424) | copy-start | bytes 6389764
  304.6 90.6 %copy-start.57 = (f32[520]{0:T(1024)}, f32[520]{0:T(1024)S(1)}, u32[]{:S(2)}) copy-start(f32[520]{0:T(1024)S(1)} %broadcast_multiply_fusion.2) | copy-start | bytes 6244
  305.0 90.2 %copy-start.53 = (f32[520]{0:T(1024)}, f32[520]{0:T(1024)S(1)}, u32[]{:S(2)}) copy-start(f32[520]{0:T(1024)S(1)} %multiply_reduce_fusion.4) | copy-start | bytes 6244
  305.0 90.2 %copy-start.84 = (f32[520]{0:T(1024)}, f32[520]{0:T(1024)S(1)}, u32[]{:S(2)}) copy-start(f32[520]{0:T(1024)S(1)} %fusion.200) | copy-start | bytes 6244
  395.2 11.6 copy-start.119
  395.3 98.6 %copy-start.81 = (f32[1,1,1024]{2,0,1:T(1,128)S(1)}, f32[1,1,1024]{2,0,1:T(1,128)}, u32[]{:S(2)}) copy-start(f32[1,1,1024]{2,0,1:T(1,128)} %get-tuple-element.453) | copy-start | bytes 12292
  395.3 98.6 %copy-start.93 = (f32[3072]{0:T(1024)S(1)}, f32[3072]{0:T(1024)}, u32[]{:S(2)}) copy-start(f32[3072]{0:T(1024)} %get-tuple-element.473) | copy-start | bytes 36868
  395.3 98.6 %copy-start.108 = (f32[1,1,1024]{2,0,1:T(1,128)S(1)}, f32[1,1,1024]{2,0,1:T(1,128)}, u32[]{:S(2)}) copy-start(f32[1,1,1024]{2,0,1:T(1,128)} %get-tuple-element.454) | copy-start | bytes 12292
  406.8 240.9 %copy-start.5 = (f32[1,520,1024]{2,1,0:T(8,128)}, f32[1,520,1024]{2,1,0:T(8,128)S(1)}, u32[]{:S(2)}) copy-start(f32[1,520,1024]{2,1,0:T(8,128)S(1)} %get-tuple-element.420) | copy-start | bytes 6389764
  406.8 95.1 %copy-start.59 = (f32[520]{0:T(1024)}, f32[520]{0:T(1024)S(1)}, u32[]{:S(2)}) copy-start(f32[520]{0:T(1024)S(1)} %broadcast_multiply_fusion.1) | copy-start | bytes 6244
  407.2 94.8 %copy-start.55 = (f32[520]{0:T(1024)}, f32[520]{0:T(1024)S(1)}, u32[]{:S(2)}) copy-start(f32[520]{0:T(1024)S(1)} %multiply_reduce_fusion.3) | copy-start | bytes 6244
  407.2 94.7 %copy-start.86 = (f32[520]{0:T(1024)}, f32[520]{0:T(1024)S(1)}, u32[]{:S(2)}) copy-start(f32[520]{0:T(1024)S(1)} %fusion.201) | copy-start | bytes 6244
  621.7 13.1 copy-start.39
  621.7 13.1 copy-start.41
  647.8 74.5 %copy-start.74 = (f32[1,4,1024]{2,0,1:T(1,128)S(1)}, f32[1,4,1024]{2,0,1:T(1,128)}, u32[]{:S(2)}) copy-start(f32[1,4,1024]{2,0,1:T(1,128)} %slice.281) | copy-start | bytes 49156
  647.8 74.5 %copy-start.75 = (f32[1,1,1024]{2,0,1:T(1,128)S(1)}, f32[1,1,1024]{2,0,1:T(1,128)}, u32[]{:S(2)}) copy-start(f32[1,1,1024]{2,0,1:T(1,128)} %get-tuple-element.449) | copy-start | bytes 12292
  647.8 74.5 %copy-start.102 = (f32[1,1,1024]{2,0,1:T(1,128)S(1)}, f32[1,1,1024]{2,0,1:T(1,128)}, u32[]{:S(2)}) copy-start(f32[1,1,1024]{2,0,1:T(1,128)} %get-tuple-element.450) | copy-start | bytes 12292
  652.6 122.0 %copy-start.62 = (f32[520]{0:T(1024)}, f32[520]{0:T(1024)S(1)}, u32[]{:S(2)}) copy-start(f32[520]{0:T(1024)S(1)} %broadcast_multiply_fusion) | copy-start | bytes 6244
  654.4 120.1 %copy-start.89 = (f32[520]{0:T(1024)}, f32[520]{0:T(1024)S(1)}, u32[]{:S(2)}) copy-start(f32[520]{0:T(1024)S(1)} %fusion.202) | copy-start | bytes 6244
  722.3 28.1 %copy-start.34 = (bf16[1,520,1024]{2,1,0:T(8,128)(2,1)S(1)}, bf16[1,520,1024]{2,1,0:T(8,128)(2,1)}, u32[]{:S(2)}) copy-start(bf16[1,520,1024]{2,1,0:T(8,128)(2,1)} %param.25) | copy-start | bytes 3194884
  722.3 28.1 %copy-start.79 = (f32[1,1,1024]{2,0,1:T(1,128)S(1)}, f32[1,1,1024]{2,0,1:T(1,128)}, u32[]{:S(2)}) copy-start(f32[1,1,1024]{2,0,1:T(1,128)} %get-tuple-element.447) | copy-start | bytes 12292
  750.4 14.6 copy-start.9
  937.0 14.5 copy-start.71
  952.4 14.3 copy-start.37
  952.4 14.3 copy-start.20
  952.4 14.3 copy-start.58
  952.4 14.3 copy-start.78
  952.4 14.3 copy-start.85
  966.7 10.1 copy-start.121
  966.7 10.1 copy-start.54
  1147.4 299.8 %reduce-scatter.13.cloned.1.call-start = ((), (), s32[]{:S(2)}) async-start(), calls=%async_computation.15 | async-start | bytes 9437184 | tf_op jit(solution)/shard_map/reduce_scatter | solution.py:292
  1167.9 564.9 %reduce-scatter.15.cloned.1.call-start = ((), (), s32[]{:S(2)}) async-start(), calls=%async_computation.16 | async-start | bytes 18874368 | tf_op jit(solution)/shard_map/reduce_scatter | solution.py:295
  1193.3 825.6 %reduce-scatter.17.cloned.1.call-start = ((), (), s32[]{:S(2)}) async-start(), calls=%async_computation.17 | async-start | bytes 18874368 | tf_op jit(solution)/shard_map/reduce_scatter | solution.py:295
  1219.5 863.6 %reduce-scatter.19.cloned.1.call-start = ((), (), s32[]{:S(2)}) async-start(), calls=%async_computation.22 | async-start | bytes 294912
  1234.0 913.1 %reduce-scatter.21.cloned.1.call-start = ((), (), s32[]{:S(2)}) async-start(), calls=%async_computation.23 | async-start | bytes 294912
  1237.6 781.4 %copy-start.13 = (f32[520,1024]{1,0:T(8,128)S(1)}, f32[520,1024]{1,0:T(8,128)}, u32[]{:S(2)}) copy-start(f32[520,1024]{1,0:T(8,128)} %copy-done.12) | copy-start | bytes 6389764
  1237.6 781.4 %copy-start.18 = (bf16[1,520,1024]{2,1,0:T(8,128)(2,1)S(1)}, bf16[1,520,1024]{2,1,0:T(8,128)(2,1)}, u32[]{:S(2)}) copy-start(bf16[1,520,1024]{2,1,0:T(8,128)(2,1)} %param.20) | copy-start | bytes 3194884
  1237.6 1031.3 %all-reduce.4.cloned.1.call-start = ((), (), s32[]{:S(2)}) async-start(), calls=%async_computation.24 | async-start | bytes 12582912 | tf_op jit(solution)/shard_map/psum | solution.py:303
  2019.0 134.8 %copy-start.47 = (bf16[2,14,128]{2,0,1:T(2,128)(2,1)S(1)}, bf16[2,14,128]{2,0,1:T(2,128)(2,1)}, u32[]{:S(2)}) copy-start(bf16[2,14,128]{2,0,1:T(2,128)(2,1)} %param.24) | copy-start | bytes 21508
  2019.0 134.8 %copy-start.91 = (f32[2,14,128]{2,0,1:T(2,128)S(1)}, f32[2,14,128]{2,0,1:T(2,128)}, u32[]{:S(2)}) copy-start(f32[2,14,128]{2,0,1:T(2,128)} %param.30) | copy-start | bytes 43012
  2019.0 134.8 %copy-start.92 = (f32[2,14,128]{2,0,1:T(2,128)S(1)}, f32[2,14,128]{2,0,1:T(2,128)}, u32[]{:S(2)}) copy-start(f32[2,14,128]{2,0,1:T(2,128)} %param.31) | copy-start | bytes 43012
  2268.9 19.0 copy-start.27
  2268.9 19.1 copy-start.38
  (83 other events, 363.0 us)
Sparse Core Ops, SparseCore 0:
  10.7 128.7 all-gather.10
  142.2 225.7 all-gather.12
  370.8 123.1 all-gather.14
  496.5 225.7 all-gather.16
  1147.5 147.1 reduce-scatter.10
  1299.2 147.9 reduce-scatter.12
  1451.0 281.8 reduce-scatter.14
  1737.1 281.7 reduce-scatter.16
  2022.8 60.2 reduce-scatter.18
  2086.8 60.2 reduce-scatter.20
  2149.7 119.1 all-reduce.3
where the time goes:
time: 2320 us; the launch traced here: 2300 us
  waiting for transfers between devices  1320 us (57%)
  matrix products  486 us (21%)
  local copies, waits for them, and re-layouts  247 us (11%)
  other arithmetic  136 us (6%)
  blocking collectives  101 us (4%)
    reduce_scatter x2, waiting for transfers between devices, local(): lax.psum_scatter(local_grads[1].astype(jnp.bfloat16), 'fsdp', scatter_dim...  572 us
    reduce_scatter x2, waiting for transfers between devices, local(): lax.psum_scatter(local_grads[0].astype(jnp.bfloat16), 'fsdp', scatter_dim...  209 us
    dot_general x56, matrix products, contract_last(): lax.dot_general(left_side, right_side, (((left_side.ndim - 1,), (1,)), ((...  176 us
    all_gather x2, waiting for transfers between devices, local(): lax.all_gather(attn_weights[layer_index], 'fsdp', axis=0, tiled=True)  166 us
    all_gather x2, waiting for transfers between devices, local(): lax.all_gather(mlp_weights[layer_index], 'fsdp', axis=0, tiled=True)  131 us
    unnamed x13, waiting for transfers between devices  125 us
    psum x1, waiting for transfers between devices, local(): lax.psum(owned[0].astype(jnp.bfloat16), ('dp', 'seq')).astype(jnp.float32)  113 us
    dot_general x8, matrix products, contract_rows(): lax.dot_general(left_side, right_side, (((0, 1), (0, 1)), ((), ())), pref...  62.7 us
  transfers between devices with their start and end apart: 11, of which 11 were waited for; matrix products, arithmetic and copies ran while one was open for 17% of the time, Pallas kernels for 0%

commit v1 on v0

--- a/solution.py
+++ b/solution.py
@@ -300,7 +300,7 @@
             ).astype(jnp.float32),
         )
         owned = (
-            lax.psum(owned[0].astype(jnp.bfloat16), ("dp", "seq")).astype(jnp.float32),
+            lax.psum(lax.psum(owned[0].astype(jnp.bfloat16), "dp"), "seq").astype(jnp.float32),
             lax.psum(owned[1].astype(jnp.bfloat16), ("dp", "seq")).astype(jnp.float32),
             lax.psum(owned[2].astype(jnp.bfloat16), ("dp", "seq")).astype(jnp.float32),
         )

time: 2320 us -> 2360 us (1.017)
  waiting for transfers between devices: 1320 us -> 1360 us
    reduce_scatter x2, waiting for transfers between devices: 209 us -> 266 us  [local(): lax.psum_scatter(local_grads[0].astype(jnp.bfloat16), 'fsdp', scatter_dim...]
    psum x1 -> x3, waiting for transfers between devices: 113 us -> 96.9 us  [the longest x1 78.9 us: local(): lax.psum(owned[1].astype(jnp.bfloat16), ('dp', 'seq')).astype(jnp.float32)]
    unnamed x13 -> x15, waiting for transfers between devices: 125 us -> 126 us
  transfers between devices with their start and end apart: 11 -> 13, of which waited for: 11 -> 13; matrix products, arithmetic and copies ran while one was open for 17% -> 18% of each run, Pallas kernels for 0% -> 0%
where the time goes in v1:
time: 2360 us; the launch traced here: 2350 us
  waiting for transfers between devices  1360 us (58%)
  matrix products  488 us (21%)
  local copies, waits for them, and re-layouts  249 us (11%)
  other arithmetic  136 us (6%)
  blocking collectives  101 us (4%)
    reduce_scatter x2, waiting for transfers between devices, local(): lax.psum_scatter(local_grads[1].astype(jnp.bfloat16), 'fsdp', scatter_dim...  572 us
    reduce_scatter x2, waiting for transfers between devices, local(): lax.psum_scatter(local_grads[0].astype(jnp.bfloat16), 'fsdp', scatter_dim...  266 us
    dot_general x56, matrix products, contract_last(): lax.dot_general(left_side, right_side, (((left_side.ndim - 1,), (1,)), ((...  176 us
    all_gather x2, waiting for transfers between devices, local(): lax.all_gather(attn_weights[layer_index], 'fsdp', axis=0, tiled=True)  166 us
    all_gather x2, waiting for transfers between devices, local(): lax.all_gather(mlp_weights[layer_index], 'fsdp', axis=0, tiled=True)  131 us
    unnamed x15, waiting for transfers between devices  126 us
    psum x1, waiting for transfers between devices, local(): lax.psum(owned[1].astype(jnp.bfloat16), ('dp', 'seq')).astype(jnp.float32)  78.9 us
    dot_general x8, matrix products, contract_rows(): lax.dot_general(left_side, right_side, (((0, 1), (0, 1)), ((), ())), pref...  64.7 us
  transfers between devices with their start and end apart: 13, of which 13 were waited for; matrix products, arithmetic and copies ran while one was open for 18% of the time, Pallas kernels for 0%

profile of v1, /device:TPU:0, one launch (start us, length us, event | category | flops | bytes accessed | tf_op | source)
XLA Modules:
  0.0 2350.7 jit_solution(13678598487474144911)
XLA Ops:
  16.5 23.2 all-gather
  39.9 17.4 all-gather.3
  59.9 79.7 %all-gather.11.cloned.1.call-done = bf16[1,1024,4096]{2,1,0:T(8,128)(2,1)} async-done(((bf16[1,128,4096]{2,1,0:T(8,128)(2,1)}), bf16[1,1024,4096]{2,1,0:T(8,128)(2,1)}) %all-gather.11.cloned.1.call-update) | async-done | bytes 8388624 | tf_op jit(solution)/shard_map/all_gather | solution.py:271
  139.5 8.1 add_convert_fusion.3
  147.6 8.5 reshape.862
  158.6 7.5 all_to_all.120
  166.1 10.3 copy.103
  176.4 8.6 reshape.863
  198.8 72.4 %while.44 = (s32[]{:T(128)}, bf16[8,1040,64]{1,2,0:T(8,128)(2,1)}, f32[8,1040]{1,0:T(8,128)S(1)}, s32[8,1040]{1,0:T(8,128)S(1)}, bf16[8,1040,64]{2,1,0:T(8,128)(...) while((s32[]{:T(128)}, bf16[8,1040,64]{1,2,0:T(8,128)(2,1)}, ...), condition=%wide.region_5.6_spmd, body=%wide.region_2.5_spmd.sunk | while | flops 285608960 | bytes 31756240 | solution.py:110
  271.3 6.4 copy.107
  278.2 8.9 reduce.63
  289.4 7.1 all_to_all.121
  299.9 4.7 fusion.226
  305.1 63.0 %all-gather.13.cloned.1.call-done = bf16[1,1024,8192]{2,1,0:T(8,128)(2,1)} async-done(((bf16[1,128,8192]{2,1,0:T(8,128)(2,1)}), bf16[1,1024,8192]{2,1,0:T(8,128)(2,1)}) %all-gather.13.cloned.1.call-update) | async-done | bytes 16777232 | tf_op jit(solution)/shard_map/all_gather | solution.py:272
  368.1 27.0 %multiply_convert_fusion.3 = (bf16[520,4096]{1,0:T(8,128)(2,1)S(1)}, f32[520,4096]{1,0:T(8,128)}, f32[520,4096]{1,0:T(8,128)}) fusion(f32[4096]{0:T(1024)S(1)} %bitcast.487, bf16[1024,8192]{1,0:T(8,128)(2,1)} %bitcast.522, f32[1,520,1024]{2,1,0:T(8,128)S(1)} %get-tuple-element.426, f32[1024]{0:T(1024)S(1)} %bitcast.513, f32[1024]{0:T(1024)S(1)} %bitcast.503, ...), kind=kOutput, calls=%fused_computation.138 | convolution fusion | flops 4505313280 | bytes 31846464 | tf_op jit(solution)/shard_map/dot_general | solution.py:122
  395.2 11.5 fusion.224
  407.2 86.8 %all-gather.15.cloned.1.call-done = bf16[1,1024,4096]{2,1,0:T(8,128)(2,1)} async-done(((bf16[1,128,4096]{2,1,0:T(8,128)(2,1)}), bf16[1,1024,4096]{2,1,0:T(8,128)(2,1)}) %all-gather.15.cloned.1.call-update) | async-done | bytes 8388624 | tf_op jit(solution)/shard_map/all_gather | solution.py:271
  493.9 8.0 add_convert_fusion.2
  502.0 8.6 reshape.869
  513.0 7.5 all_to_all.122
  520.5 10.2 copy.110
  530.7 8.6 reshape.870
  552.9 68.8 %while.45 = (s32[]{:T(128)}, bf16[8,1040,64]{1,2,0:T(8,128)(2,1)S(1)}, f32[8,1040]{1,0:T(8,128)S(1)}, s32[8,1040]{1,0:T(8,128)S(1)}, bf16[8,1040,64]{2,1,0:T(8,1...) while((s32[]{:T(128)}, ...), condition=%wide.region_13.14_spmd, body=%wide.region_10.13_spmd.sunk | while | flops 285608960 | bytes 31763296 | solution.py:110
  625.8 8.9 reduce.64
  636.2 5.6 all_to_all.123
  654.4 67.9 %all-gather.17.cloned.1.call-done = bf16[1,1024,8192]{2,1,0:T(8,128)(2,1)} async-done(((bf16[1,128,8192]{2,1,0:T(8,128)(2,1)}), bf16[1,1024,8192]{2,1,0:T(8,128)(2,1)}) %all-gather.17.cloned.1.call-update) | async-done | bytes 16777232 | tf_op jit(solution)/shard_map/all_gather | solution.py:272
  722.3 28.0 %multiply_convert_fusion.2 = (bf16[520,4096]{1,0:T(8,128)(2,1)}, f32[520,4096]{1,0:T(8,128)}, f32[520,4096]{1,0:T(8,128)}) fusion(f32[4096]{0:T(1024)S(1)} %bitcast.489, bf16[1024,8192]{1,0:T(8,128)(2,1)} %bitcast.526, f32[1,520,1024]{2,1,0:T(8,128)} %copy-done.8, f32[1024]{0:T(1024)S(1)} %bitcast.511, f32[1024]{0:T(1024)S(1)} %bitcast.495, ...), kind=kOutput, calls=%fused_computation.125 | convolution fusion | flops 4505313280 | bytes 31846464 | tf_op jit(solution)/shard_map/dot_general | solution.py:122
  750.4 14.5 fusion.234
  764.9 9.6 fusion.153
  792.1 99.1 %while.46 = (s32[]{:T(128)}, bf16[8,3,1040,64]{2,3,1,0:T(8,128)(2,1)S(1)}, s32[8,1040]{1,0:T(8,128)}, bf16[8,1040,64]{2,1,0:T(8,128)(2,1)}, bf16[8,1040,64]{2,1,...) while((s32[]{:T(128)}, ...), condition=%wide.region_20.21_spmd, body=%wide.region_18.20_spmd.sunk | while | flops 703489280 | bytes 35388936 | solution.py:198
  893.4 8.4 copy.123
  901.8 8.7 all_to_all.125
  917.2 8.5 reshape.882
  925.7 7.9 fusion.155
  937.0 14.5 fusion.152
  952.4 14.3 fusion.235
  966.8 10.0 fusion.157
  997.2 99.1 %while.47 = (s32[]{:T(128)}, bf16[8,3,1040,64]{2,3,1,0:T(8,128)(2,1)S(1)}, s32[8,1040]{1,0:T(8,128)}, bf16[8,1040,64]{2,1,0:T(8,128)(2,1)}, bf16[8,1040,64]{2,1,...) while((s32[]{:T(128)}, ...), condition=%wide.region_27.28_spmd, body=%wide.region_25.27_spmd.sunk | while | flops 703489280 | bytes 35388936 | solution.py:198
  1098.5 8.4 copy.133
  1106.9 8.7 all_to_all.127
  1122.2 8.4 reshape.890
  1130.7 9.4 convolution_convert_fusion.5
  1140.1 7.0 pad_maximum_fusion.2
  1147.3 4.9 convolution_convert_fusion.6
  1152.2 7.7 convolution_convert_fusion.4
  1159.9 7.8 pad_maximum_fusion.3
  1169.3 11.6 convolution_convert_fusion.3
  1180.8 113.6 %reduce-scatter.11.cloned.1.call-done = bf16[128,4096]{1,0:T(8,128)(2,1)} async-done(((bf16[1024,4096]{1,0:T(8,128)(2,1)}), bf16[128,4096]{1,0:T(8,128)(2,1)}) %reduce-scatter.11.cloned.1.call-update) | async-done | bytes 1048592 | tf_op jit(solution)/shard_map/reduce_scatter | solution.py:292
  1294.5 152.5 %reduce-scatter.13.cloned.1.call-done = bf16[128,4096]{1,0:T(8,128)(2,1)} async-done(((bf16[1024,4096]{1,0:T(8,128)(2,1)}), bf16[128,4096]{1,0:T(8,128)(2,1)}) %reduce-scatter.13.cloned.1.call-update) | async-done | bytes 1048592 | tf_op jit(solution)/shard_map/reduce_scatter | solution.py:292
  1447.1 9.0 convolution_convert_fusion.2
  1456.1 6.6 pad_maximum_fusion
  1463.5 9.3 convolution_convert_fusion
  1472.8 9.6 convolution_convert_fusion.1
  1482.4 6.7 pad_maximum_fusion.1
  1489.2 6.9 fusion.150
  1511.7 286.7 %reduce-scatter.15.cloned.1.call-done = bf16[128,8192]{1,0:T(8,128)(2,1)} async-done(((bf16[1024,8192]{1,0:T(8,128)(2,1)}), bf16[128,8192]{1,0:T(8,128)(2,1)}) %reduce-scatter.15.cloned.1.call-update) | async-done | bytes 2097168 | tf_op jit(solution)/shard_map/reduce_scatter | solution.py:295
  1798.4 285.6 %reduce-scatter.17.cloned.1.call-done = bf16[128,8192]{1,0:T(8,128)(2,1)} async-done(((bf16[1024,8192]{1,0:T(8,128)(2,1)}), bf16[128,8192]{1,0:T(8,128)(2,1)}) %reduce-scatter.17.cloned.1.call-update) | async-done | bytes 2097168 | tf_op jit(solution)/shard_map/reduce_scatter | solution.py:295
  2087.7 60.7 %reduce-scatter.19.cloned.1.call-done = bf16[128,14]{1,0:T(8,128)(2,1)} async-done(((bf16[1024,14]{1,0:T(8,128)(2,1)}), bf16[128,14]{1,0:T(8,128)(2,1)}) %reduce-scatter.19.cloned.1.call-update) | async-done | bytes 3600
  2149.3 63.8 %reduce-scatter.21.cloned.1.call-done = bf16[128,14]{1,0:T(8,128)(2,1)} async-done(((bf16[1024,14]{1,0:T(8,128)(2,1)}), bf16[128,14]{1,0:T(8,128)(2,1)}) %reduce-scatter.21.cloned.1.call-update) | async-done | bytes 3600
  2213.9 5.8 all-reduce
  2222.2 13.6 all-reduce.10.cloned.1.call-done
  2235.8 10.4 add_multiply_fusion.1
  2246.2 78.9 %all-reduce.8.cloned.1.call-done = (bf16[1,128,8192]{2,1,0:T(8,128)(2,1)}, bf16[1,128,8192]{2,1,0:T(8,128)(2,1)}) async-done(((bf16[1,128,8192]{2,1,0:T(8,128)(2,1)}, bf16[1,128,8192]{2,1,0:T(8,128)(2,1)}), (bf16[1,128,8192]{2,1,0:T(8,128)(2,1)}, bf16[1,128,8192]{2,1,0:T(8,128)(2,1)})) %all-reduce.8.cloned.1.call-update) | async-done | bytes 4194320 | tf_op jit(solution)/shard_map/psum | solution.py:304
  2325.1 18.9 add_multiply_fusion
  (684 shorter events, 492.2 us)
Async XLA Ops:
  7.2 132.3 %all-gather.11.cloned.1.call-start = ((), (), s32[]{:S(2)}) async-start(), calls=%async_computation.18 | async-start | bytes 9437184 | tf_op jit(solution)/shard_map/all_gather | solution.py:271
  10.3 357.7 %all-gather.13.cloned.1.call-start = ((), (), s32[]{:S(2)}) async-start(), calls=%async_computation.19 | async-start | bytes 18874368 | tf_op jit(solution)/shard_map/all_gather | solution.py:272
  15.1 43.5 %copy-start.16 = (bf16[1,520,1024]{2,1,0:T(8,128)(2,1)S(1)}, bf16[1,520,1024]{2,1,0:T(8,128)(2,1)}, u32[]{:S(2)}) copy-start(bf16[1,520,1024]{2,1,0:T(8,128)(2,1)} %param.20) | copy-start | bytes 3194884
  15.1 44.1 %copy-start.100 = (s32[1,1040]{1,0:T(1,128)S(1)}, s32[1,1040]{1,0:T(1,128)}, u32[]{:S(2)}) copy-start(s32[1,1040]{1,0:T(1,128)} %param.21) | copy-start | bytes 12484
  15.1 478.8 %all-gather.15.cloned.1.call-start = ((), (), s32[]{:S(2)}) async-start(), calls=%async_computation.20 | async-start | bytes 9437184 | tf_op jit(solution)/shard_map/all_gather | solution.py:271
  15.8 706.5 %all-gather.17.cloned.1.call-start = ((), (), s32[]{:S(2)}) async-start(), calls=%async_computation.21 | async-start | bytes 18874368 | tf_op jit(solution)/shard_map/all_gather | solution.py:272
  16.4 1278.1 %reduce-scatter.11.cloned.1.call-start = ((), (), s32[]{:S(2)}) async-start(), calls=%async_computation.14 | async-start | bytes 9437184 | tf_op jit(solution)/shard_map/reduce_scatter | solution.py:292
  39.7 107.9 %copy-start.48 = (f32[1,1,1024]{2,0,1:T(1,128)}, f32[1,1,1024]{2,0,1:T(1,128)S(1)}, u32[]{:S(2)}) copy-start(f32[1,1,1024]{2,0,1:T(1,128)S(1)} %get-tuple-element.465) | copy-start | bytes 12292
  39.8 107.8 %copy-start.105 = (f32[1,1,1024]{2,0,1:T(1,128)}, f32[1,1,1024]{2,0,1:T(1,128)S(1)}, u32[]{:S(2)}) copy-start(f32[1,1,1024]{2,0,1:T(1,128)S(1)} %get-tuple-element.466) | copy-start | bytes 12292
  39.8 260.1 %copy-start.65 = (f32[1,1,1024]{2,0,1:T(1,128)}, f32[1,1,1024]{2,0,1:T(1,128)S(1)}, u32[]{:S(2)}) copy-start(f32[1,1,1024]{2,0,1:T(1,128)S(1)} %get-tuple-element.463) | copy-start | bytes 12292
  39.8 260.1 %copy-start.67 = (f32[1,1,1024]{2,0,1:T(1,128)}, f32[1,1,1024]{2,0,1:T(1,128)S(1)}, u32[]{:S(2)}) copy-start(f32[1,1,1024]{2,0,1:T(1,128)S(1)} %get-tuple-element.464) | copy-start | bytes 12292
  39.8 328.3 %copy-start.78 = (f32[1,1,1024]{2,0,1:T(1,128)}, f32[1,1,1024]{2,0,1:T(1,128)S(1)}, u32[]{:S(2)}) copy-start(f32[1,1,1024]{2,0,1:T(1,128)S(1)} %get-tuple-element.461) | copy-start | bytes 12292
  39.8 328.3 %copy-start.103 = (f32[1,1,1024]{2,0,1:T(1,128)}, f32[1,1,1024]{2,0,1:T(1,128)S(1)}, u32[]{:S(2)}) copy-start(f32[1,1,1024]{2,0,1:T(1,128)S(1)} %get-tuple-element.462) | copy-start | bytes 12292
  39.8 355.4 %copy-start.69 = (f32[1,1,1024]{2,0,1:T(1,128)}, f32[1,1,1024]{2,0,1:T(1,128)S(1)}, u32[]{:S(2)}) copy-start(f32[1,1,1024]{2,0,1:T(1,128)S(1)} %get-tuple-element.459) | copy-start | bytes 12292
  39.8 355.4 %copy-start.109 = (f32[1,1,1024]{2,0,1:T(1,128)}, f32[1,1,1024]{2,0,1:T(1,128)S(1)}, u32[]{:S(2)}) copy-start(f32[1,1,1024]{2,0,1:T(1,128)S(1)} %get-tuple-element.460) | copy-start | bytes 12292
  39.9 328.2 %copy-start.71 = (f32[1,4,1024]{2,0,1:T(1,128)}, f32[1,4,1024]{2,0,1:T(1,128)S(1)}, u32[]{:S(2)}) copy-start(f32[1,4,1024]{2,0,1:T(1,128)S(1)} %slice.263) | copy-start | bytes 49156
  58.8 88.9 %copy-start.41 = (f32[520]{0:T(1024)}, f32[520]{0:T(1024)S(1)}, u32[]{:S(2)}) copy-start(f32[520]{0:T(1024)S(1)} %broadcast_multiply_fusion.3) | copy-start | bytes 6244
  59.2 88.4 %copy-start.50 = (f32[520]{0:T(1024)}, f32[520]{0:T(1024)S(1)}, u32[]{:S(2)}) copy-start(f32[520]{0:T(1024)S(1)} %fusion.149) | copy-start | bytes 6244
  59.2 88.4 %copy-start.43 = (f32[520]{0:T(1024)}, f32[520]{0:T(1024)S(1)}, u32[]{:S(2)}) copy-start(f32[520]{0:T(1024)S(1)} %fusion.199) | copy-start | bytes 6244
  271.2 15.9 copy-start.15
  271.3 15.9 copy-start.39
  304.7 90.5 %copy-start.21 = (f32[1,520,1024]{2,1,0:T(8,128)}, f32[1,520,1024]{2,1,0:T(8,128)S(1)}, u32[]{:S(2)}) copy-start(f32[1,520,1024]{2,1,0:T(8,128)S(1)} %get-tuple-element.426) | copy-start | bytes 6389764
  304.7 90.5 %copy-start.56 = (f32[520]{0:T(1024)}, f32[520]{0:T(1024)S(1)}, u32[]{:S(2)}) copy-start(f32[520]{0:T(1024)S(1)} %broadcast_multiply_fusion.2) | copy-start | bytes 6244
  305.0 90.1 %copy-start.52 = (f32[520]{0:T(1024)}, f32[520]{0:T(1024)S(1)}, u32[]{:S(2)}) copy-start(f32[520]{0:T(1024)S(1)} %multiply_reduce_fusion.4) | copy-start | bytes 6244
  305.0 90.1 %copy-start.83 = (f32[520]{0:T(1024)}, f32[520]{0:T(1024)S(1)}, u32[]{:S(2)}) copy-start(f32[520]{0:T(1024)S(1)} %fusion.200) | copy-start | bytes 6244
  395.1 11.6 copy-start.118
  395.2 98.7 %copy-start.80 = (f32[1,1,1024]{2,0,1:T(1,128)S(1)}, f32[1,1,1024]{2,0,1:T(1,128)}, u32[]{:S(2)}) copy-start(f32[1,1,1024]{2,0,1:T(1,128)} %get-tuple-element.455) | copy-start | bytes 12292
  395.2 98.7 %copy-start.92 = (f32[3072]{0:T(1024)S(1)}, f32[3072]{0:T(1024)}, u32[]{:S(2)}) copy-start(f32[3072]{0:T(1024)} %get-tuple-element.475) | copy-start | bytes 36868
  395.2 98.7 %copy-start.107 = (f32[1,1,1024]{2,0,1:T(1,128)S(1)}, f32[1,1,1024]{2,0,1:T(1,128)}, u32[]{:S(2)}) copy-start(f32[1,1,1024]{2,0,1:T(1,128)} %get-tuple-element.456) | copy-start | bytes 12292
  406.7 241.0 %copy-start.5 = (f32[1,520,1024]{2,1,0:T(8,128)}, f32[1,520,1024]{2,1,0:T(8,128)S(1)}, u32[]{:S(2)}) copy-start(f32[1,520,1024]{2,1,0:T(8,128)S(1)} %get-tuple-element.422) | copy-start | bytes 6389764
  406.8 95.2 %copy-start.58 = (f32[520]{0:T(1024)}, f32[520]{0:T(1024)S(1)}, u32[]{:S(2)}) copy-start(f32[520]{0:T(1024)S(1)} %broadcast_multiply_fusion.1) | copy-start | bytes 6244
  407.1 94.8 %copy-start.54 = (f32[520]{0:T(1024)}, f32[520]{0:T(1024)S(1)}, u32[]{:S(2)}) copy-start(f32[520]{0:T(1024)S(1)} %multiply_reduce_fusion.3) | copy-start | bytes 6244
  407.1 94.8 %copy-start.85 = (f32[520]{0:T(1024)}, f32[520]{0:T(1024)S(1)}, u32[]{:S(2)}) copy-start(f32[520]{0:T(1024)S(1)} %fusion.201) | copy-start | bytes 6244
  621.6 13.1 copy-start.38
  621.7 13.1 copy-start.40
  647.8 74.5 %copy-start.73 = (f32[1,4,1024]{2,0,1:T(1,128)S(1)}, f32[1,4,1024]{2,0,1:T(1,128)}, u32[]{:S(2)}) copy-start(f32[1,4,1024]{2,0,1:T(1,128)} %slice.281) | copy-start | bytes 49156
  647.8 74.5 %copy-start.74 = (f32[1,1,1024]{2,0,1:T(1,128)S(1)}, f32[1,1,1024]{2,0,1:T(1,128)}, u32[]{:S(2)}) copy-start(f32[1,1,1024]{2,0,1:T(1,128)} %get-tuple-element.451) | copy-start | bytes 12292
  647.8 74.5 %copy-start.101 = (f32[1,1,1024]{2,0,1:T(1,128)S(1)}, f32[1,1,1024]{2,0,1:T(1,128)}, u32[]{:S(2)}) copy-start(f32[1,1,1024]{2,0,1:T(1,128)} %get-tuple-element.452) | copy-start | bytes 12292
  652.5 122.0 %copy-start.61 = (f32[520]{0:T(1024)}, f32[520]{0:T(1024)S(1)}, u32[]{:S(2)}) copy-start(f32[520]{0:T(1024)S(1)} %broadcast_multiply_fusion) | copy-start | bytes 6244
  654.4 120.2 %copy-start.88 = (f32[520]{0:T(1024)}, f32[520]{0:T(1024)S(1)}, u32[]{:S(2)}) copy-start(f32[520]{0:T(1024)S(1)} %fusion.202) | copy-start | bytes 6244
  722.3 28.1 %copy-start.34 = (bf16[1,520,1024]{2,1,0:T(8,128)(2,1)S(1)}, bf16[1,520,1024]{2,1,0:T(8,128)(2,1)}, u32[]{:S(2)}) copy-start(bf16[1,520,1024]{2,1,0:T(8,128)(2,1)} %param.25) | copy-start | bytes 3194884
  722.3 28.1 %copy-start.76 = (f32[1,1,1024]{2,0,1:T(1,128)S(1)}, f32[1,1,1024]{2,0,1:T(1,128)}, u32[]{:S(2)}) copy-start(f32[1,1,1024]{2,0,1:T(1,128)} %get-tuple-element.449) | copy-start | bytes 12292
  750.4 14.6 copy-start.9
  937.0 14.5 copy-start.70
  952.4 14.3 copy-start.37
  952.4 14.3 copy-start.22
  952.4 14.3 copy-start.57
  952.4 14.3 copy-start.79
  952.4 14.3 copy-start.84
  966.7 10.0 copy-start.120
  966.7 10.0 copy-start.53
  1147.2 299.8 %reduce-scatter.13.cloned.1.call-start = ((), (), s32[]{:S(2)}) async-start(), calls=%async_computation.15 | async-start | bytes 9437184 | tf_op jit(solution)/shard_map/reduce_scatter | solution.py:292
  1167.7 343.8 %all-reduce.12.cloned.1.call-start = ((), (), s32[]{:S(2)}) async-start(), calls=%async_computation.26 | async-start | bytes 4194304 | tf_op jit(solution)/shard_map/psum | solution.py:303
  1447.0 351.4 %reduce-scatter.15.cloned.1.call-start = ((), (), s32[]{:S(2)}) async-start(), calls=%async_computation.16 | async-start | bytes 18874368 | tf_op jit(solution)/shard_map/reduce_scatter | solution.py:295
  1462.8 621.2 %reduce-scatter.17.cloned.1.call-start = ((), (), s32[]{:S(2)}) async-start(), calls=%async_computation.17 | async-start | bytes 18874368 | tf_op jit(solution)/shard_map/reduce_scatter | solution.py:295
  1489.1 659.3 %reduce-scatter.19.cloned.1.call-start = ((), (), s32[]{:S(2)}) async-start(), calls=%async_computation.22 | async-start | bytes 294912
  1503.6 709.5 %reduce-scatter.21.cloned.1.call-start = ((), (), s32[]{:S(2)}) async-start(), calls=%async_computation.23 | async-start | bytes 294912
  1507.0 577.1 %copy-start.13 = (f32[520,1024]{1,0:T(8,128)S(1)}, f32[520,1024]{1,0:T(8,128)}, u32[]{:S(2)}) copy-start(f32[520,1024]{1,0:T(8,128)} %copy-done.12) | copy-start | bytes 6389764
  1507.0 577.1 %copy-start.18 = (bf16[1,520,1024]{2,1,0:T(8,128)(2,1)S(1)}, bf16[1,520,1024]{2,1,0:T(8,128)(2,1)}, u32[]{:S(2)}) copy-start(bf16[1,520,1024]{2,1,0:T(8,128)(2,1)} %param.20) | copy-start | bytes 3194884
  1507.0 728.8 %all-reduce.10.cloned.1.call-start = ((), (), s32[]{:S(2)}) async-start(), calls=%async_computation.25 | async-start | bytes 4194304 | tf_op jit(solution)/shard_map/psum | solution.py:303
  1511.5 813.6 %all-reduce.8.cloned.1.call-start = ((), (), s32[]{:S(2)}) async-start(), calls=%async_computation.24 | async-start | bytes 8388608 | tf_op jit(solution)/shard_map/psum | solution.py:304
  2084.1 135.6 %copy-start.46 = (bf16[2,14,128]{2,0,1:T(2,128)(2,1)S(1)}, bf16[2,14,128]{2,0,1:T(2,128)(2,1)}, u32[]{:S(2)}) copy-start(bf16[2,14,128]{2,0,1:T(2,128)(2,1)} %param.24) | copy-start | bytes 21508
  2084.1 135.6 %copy-start.90 = (f32[2,14,128]{2,0,1:T(2,128)S(1)}, f32[2,14,128]{2,0,1:T(2,128)}, u32[]{:S(2)}) copy-start(f32[2,14,128]{2,0,1:T(2,128)} %param.30) | copy-start | bytes 43012
  2084.1 135.6 %copy-start.91 = (f32[2,14,128]{2,0,1:T(2,128)S(1)}, f32[2,14,128]{2,0,1:T(2,128)}, u32[]{:S(2)}) copy-start(f32[2,14,128]{2,0,1:T(2,128)} %param.31) | copy-start | bytes 43012
  (84 other events, 355.5 us)
Sparse Core Ops, SparseCore 0:
  10.7 128.7 all-gather.10
  142.2 225.7 all-gather.12
  370.8 123.1 all-gather.14
  496.5 225.7 all-gather.16
  1147.3 147.1 reduce-scatter.10
  1299.0 147.9 reduce-scatter.12
  1449.4 62.0 all-reduce.11
  1515.7 282.6 reduce-scatter.14
  1802.2 281.7 reduce-scatter.16
  2088.1 60.3 reduce-scatter.18
  2152.8 60.2 reduce-scatter.20
  2215.4 20.3 all-reduce.9
  2238.2 86.8 all-reduce.7
